TPU v7x, 512 devices: a whole 4x8x8 slice. The times are simulated.
512 devices in a mesh: mod: 2 (over z_hi), loop: 16 (over x, z_lo), line: 16 (over y, core).
Axes of the slice: x: 4, y: 8, z: 8 (z_hi: 2, z_lo: 4; z = z_hi * 4 + z_lo), core: 2. Of those that a mesh axis runs over, the one named last changes fastest.
Arguments:
- act: bfloat16 [2, 196608, 512], P('mod', ('loop', 'line'))
- dy: bfloat16 [2, 196608, 1280], P('mod', ('loop', 'line')), may hold values from -6 to 6
- w_out: bfloat16 [2, 512, 1280], P('mod'), may hold values from -0.15625 to 0.15625
- counts: int32 [2, 16, 16], P('mod', 'loop', 'line'), may hold values from 192 to 768, as said below
Outputs:
- grad_clipped: float32 [2, 512, 1280], P('mod', 'loop')
- hidden_grad: bfloat16 [2, 196608, 512], P('mod', ('loop', 'line'))
Inputs may be any that keep to these rules, and one draw needn't show every extreme that they name: `counts`: in each tower some device has all 768 slots live.
All inputs are finite; a program needn't handle non-finite values.
Results may differ from a plain program's by a relative error of at most 0.001.
Values sent between devices are 32-bit elements; how exact they have to be, the bound alone decides.
A program may use at most 64 MiB of HBM per device.

v0:
```python
import jax
import jax.numpy as jnp
from jax import lax
from jax.sharding import PartitionSpec as P


def on_device(act, dy, w_out, counts):
    tokens = act[0]
    upstream = dy[0]
    weight = w_out[0]
    rows = tokens.shape[0]
    hidden = tokens.shape[1]
    block = weight.shape[1]
    live = lax.broadcasted_iota(jnp.int32, (rows, 1), 0) < counts[0, 0]
    masked = jnp.where(live, tokens, jnp.zeros_like(tokens))
    entries = lax.axis_size("mod") * hidden * block
    share = lax.psum_scatter(
        lax.dot_general(
            masked, upstream, (((0,), (0,)), ((), ())), preferred_element_type=jnp.float32
        ),
        "loop",
        scatter_dimension=0,
        tiled=True,
    )
    share = lax.psum(share, "line")
    total = lax.psum(jnp.sum(share * share), ("mod", "loop"))
    factor = 1.0 / jnp.sqrt(total / entries + 1e-06)
    clipped = share * factor
    back = lax.dot_general(
        upstream, weight, (((1,), (1,)), ((), ())), preferred_element_type=jnp.float32
    )
    hidden_grad = jnp.where(live, back, jnp.zeros_like(back)).astype(jnp.bfloat16)
    return (clipped[None], hidden_grad[None])


def solution(mesh):
    in_specs = (
        P("mod", ("loop", "line"), None),
        P("mod", ("loop", "line"), None),
        P("mod", None, None),
        P("mod", "loop", "line"),
    )
    out_specs = (P("mod", "loop", None), P("mod", ("loop", "line"), None))
    return jax.shard_map(
        on_device, mesh=mesh, in_specs=in_specs, out_specs=out_specs, check_vma=False
    )
```

profile of v0, /device:TPU:8, one launch (start us, length us, event | category | flops | bytes accessed | tf_op | source)
XLA Modules:
  0.0 310.6 jit_solution(13326542029925265666)
XLA Ops:
  7.2 0.0 copy-start
  7.2 0.0 reduce-scatter.2.cloned.1.call-start
  8.0 0.7 copy-done
  8.7 3.9 %fusion.2 = f32[512,1280]{1,0:T(8,128)} fusion(bf16[1,768,1280]{2,1,0:T(8,128)(2,1)S(1)} %copy-done, bf16[1,768,512]{2,1,0:T(8,128)(2,1)} %param.4, pred[768]{0:T(1024)(128)(4,1)S(1)} %iota_compare_fusion), kind=kOutput, calls=%fused_computation.2 | convolution fusion | flops 1007026176 | bytes 5374720 | tf_op jit(solution)/shard_map/dot_general | solution.py:18
  12.7 0.0 copy-start.2
  12.7 0.0 reduce-scatter.2.cloned.1.call-update
  12.7 0.0 all-reduce.2.cloned.1.call-start
  12.8 101.7 %reduce-scatter.2.cloned.1.call-done = f32[32,1280]{1,0:T(8,128)} async-done(((f32[512,1280]{1,0:T(8,128)}), f32[32,1280]{1,0:T(8,128)}) %reduce-scatter.2.cloned.1.call-update) | async-done | bytes 163856 | tf_op jit(solution)/shard_map/reduce_scatter | solution.py:17
  114.5 0.0 all-reduce.2.cloned.1.call-update
  114.5 108.3 %all-reduce.2.cloned.1.call-done = f32[32,1280]{1,0:T(8,128)} async-done(((f32[32,1280]{1,0:T(8,128)}), f32[32,1280]{1,0:T(8,128)}) %all-reduce.2.cloned.1.call-update) | async-done | bytes 163856 | tf_op jit(solution)/shard_map/psum | solution.py:25
  222.8 1.6 multiply_reduce_fusion
  224.4 0.0 copy-done.2
  224.4 0.0 copy-start.1
  224.4 2.1 fusion.7
  226.5 75.9 %psum.15 = f32[]{:T(128)} all-reduce(f32[]{:T(128)} %multiply_reduce_fusion), channel_id=1, replica_groups=mesh['mod'=2,'loop'=16,'line'=16] {'mod','loop'}, use_global_device_ids=true, to_apply=%region_3.4 | all-reduce | flops 1 | bytes 8 | tf_op jit(solution)/shard_map/psum | solution.py:26
  303.1 0.0 copy-done.1
  303.1 0.7 multiply_bitcast_fusion
  (1 shorter events, 0.0 us)
Async XLA Ops:
  7.2 1.6 copy-start
  7.2 107.3 %reduce-scatter.2.cloned.1.call-start = ((), (), s32[]{:S(2)}) async-start(), calls=%async_computation.1 | async-start | bytes 2785280 | tf_op jit(solution)/shard_map/reduce_scatter | solution.py:17
  12.7 211.7 %copy-start.2 = (bf16[1,512,1280]{2,1,0:T(8,128)(2,1)S(1)}, bf16[1,512,1280]{2,1,0:T(8,128)(2,1)}, u32[]{:S(2)}) copy-start(bf16[1,512,1280]{2,1,0:T(8,128)(2,1)} %param.6) | copy-start | bytes 3932164
  12.7 210.1 %all-reduce.2.cloned.1.call-start = ((), (), s32[]{:S(2)}) async-start(), calls=%async_computation.2 | async-start | bytes 327680 | tf_op jit(solution)/shard_map/psum | solution.py:25
  224.4 78.7 %copy-start.1 = (f32[32,1280]{1,0:T(8,128)S(1)}, f32[32,1280]{1,0:T(8,128)}, u32[]{:S(2)}) copy-start(f32[32,1280]{1,0:T(8,128)} %all-reduce.2.cloned.1.call-done) | copy-start | bytes 491524
Sparse Core Ops, SparseCore 0:
  12.8 101.6 reduce-scatter.1
  116.8 105.9 all-reduce.1
where the time goes:
time: 311 us
  waiting for transfers between devices  210 us (68%)
  blocking collectives  75.9 us (24%)
  between operations  15.5 us (5%)
  matrix products  6.04 us (2%)
    psum x1, waiting for transfers between devices, on_device(): share = lax.psum(share, 'line')  108 us
    reduce_scatter x1, waiting for transfers between devices, on_device(): lax.psum_scatter(lax.dot_general(masked, upstream, (((0,), (0,)), ((), ()...  102 us
    psum x1, blocking collectives, on_device(): total = lax.psum(jnp.sum(share * share), ('mod', 'loop'))  75.9 us
  transfers between devices with their start and end apart: 2, of which 2 were waited for; matrix products, arithmetic and copies ran while one was open for 0% of the time, Pallas kernels for 0%

commit v1 on v0

v1 whole, which is shorter than its diff:
```python
import functools

import jax
import jax.numpy as jnp
from jax import lax
from jax.experimental import pallas as pl
from jax.experimental.pallas import tpu as pltpu
from jax.sharding import PartitionSpec as P

MESH = pl.DeviceIdType.MESH
F32 = jnp.float32
BF16 = jnp.bfloat16

NX, NZ, NY, NM = 4, 4, 8, 2
NLINE = NY * 2
COLS = 256
UNITS = 5
SLOTS = 3


def remote(src, dst, ssem, rsem, peer):
    return pltpu.make_async_remote_copy(
        src_ref=src, dst_ref=dst, send_sem=ssem, recv_sem=rsem, device_id=peer, device_id_type=MESH
    )


def kernel(
    entries,
    cnt_ref, act_hbm, dy_hbm, w_hbm,
    out_ref, hid_hbm,
    act_v, dy_v, w_v, hid_v, act_t,
    pair_s, pair_r, own, xr, xf, zr, yr, ag, s1, s2,
    ld_sem, hid_sem,
    pair_ss, pair_rs, x_ss, x_rs, z_ss, z_rs, y_ss, y_rs,
    ag_ss, ag_rs, s1_ss, s1_rs, s2_ss, s2_rs,
):
    mod = lax.axis_index("mod")
    loop = lax.axis_index("loop")
    line = lax.axis_index("line")
    x, z = loop // NZ, lax.rem(loop, NZ)
    y, core = line // 2, lax.rem(line, 2)
    rows = act_v.shape[0]
    hidden = act_v.shape[1]

    def at(dm=0, dx=0, dz=0, dline=0):
        m2 = lax.rem(mod + dm, NM) if dm else mod
        x2 = lax.rem(x + dx, NX) if dx else x
        z2 = lax.rem(z + dz, NZ) if dz else z
        l2 = lax.rem(line + dline, NLINE) if dline else line
        return (m2, x2 * NZ + z2, l2)

    partner = (mod, loop, y * 2 + (1 - core))

    barrier = pltpu.get_barrier_semaphore()
    offsets = [(dm, dx, dz) for dm in range(NM) for dx in range(NX) for dz in range(NZ)][1:]
    for dl in range(1, NLINE):
        pl.semaphore_signal(barrier, inc=1, device_id=at(dline=dl), device_id_type=MESH)
    for dm, dx, dz in offsets:
        pl.semaphore_signal(barrier, inc=1, device_id=at(dm, dx, dz), device_id_type=MESH)

    first = 3 * (1 - core)
    mine = 3 * core
    order = [first, mine, first + 1, mine + 1, 2]
    load_act = pltpu.make_async_copy(act_hbm.at[0], act_v, ld_sem.at[0])
    load_act.start()
    load_dy = []
    for j, u in enumerate(order):
        src = dy_hbm.at[0, :, pl.ds(pl.multiple_of(u * COLS, COLS), COLS)]
        copy = pltpu.make_async_copy(src, dy_v.at[u], ld_sem.at[1 + j])
        copy.start()
        load_dy.append(copy)
    load_w = []
    for u in range(UNITS):
        src = w_hbm.at[0, :, pl.ds(u * COLS, COLS)]
        copy = pltpu.make_async_copy(src, w_v.at[u], ld_sem.at[6 + u])
        copy.start()
        load_w.append(copy)

    count = cnt_ref[0, 0, 0]
    load_act.wait()
    flipped = act_v[...].T
    alive = lax.broadcasted_iota(jnp.int32, (hidden, rows), 1) < count
    act_t[...] = jnp.where(alive, flipped, jnp.zeros_like(flipped))

    def product(u, dst):
        half = hidden // 2
        for i in range(2):
            acc = jnp.dot(act_t[i * half:(i + 1) * half, :], dy_v[u], preferred_element_type=F32)
            tiles = acc.reshape(NX // 2, NZ, 4, 8, COLS)
            dst[2 * i:2 * i + 2, :, 0:4] = tiles[..., 0:128]
            dst[2 * i:2 * i + 2, :, 4:8] = tiles[..., 128:256]

    sends = [[], [], [], []]

    def pair_copy(k):
        return remote(pair_s.at[k], pair_r.at[k], pair_ss.at[k], pair_rs.at[k], partner)

    def x_copy(k, i):
        right, left = lax.rem(x + 1, NX), lax.rem(x + 3, NX)
        across = lax.rem(x + 2, NX)
        lo, hi = pl.ds(0, 4), pl.ds(4, 4)
        src, dst, dx = (
            (own.at[k, across, :, lo], xr.at[k, 0], 1),
            (own.at[k, across, :, hi], xr.at[k, 1], 3),
            (own.at[k, right, :, hi], xf.at[k, 1], 1),
            (own.at[k, left, :, lo], xf.at[k, 2], 3),
            (own.at[k, right, :, lo], xf.at[k, 0], 1),
            (own.at[k, left, :, hi], xf.at[k, 3], 3),
        )[i]
        return remote(src, dst, x_ss.at[k, i], x_rs.at[k, i], at(dx=dx))

    def z_copy(k, d):
        src = own.at[k, x, lax.rem(z + d, NZ)]
        return remote(src, zr.at[k, d - 1], z_ss.at[k, d - 1], z_rs.at[k, d - 1], at(dz=d))

    def y_copy(k, d):
        src = own.at[k, x, z, lax.rem(y + d, NY)]
        return remote(src, yr.at[k, d - 1], y_ss.at[k, d - 1], y_rs.at[k, d - 1], at(dline=2 * d))

    def s1_copy(i):
        return remote(s1.at[0], s1.at[i + 1], s1_ss.at[i], s1_rs.at[i], at(*offsets[i]))

    def s2_copy(d):
        return remote(s2.at[0], s2.at[d], s2_ss.at[d - 1], s2_rs.at[d - 1], at(dline=d))

    def ag_copy(d):
        shard = ag.at[core, y]
        return remote(shard, shard, ag_ss.at[d - 1], ag_rs.at[d - 1], at(dline=d))

    def start(k, make, *args):
        make(*args).start()
        sends[k].append((make, args))

    def e2(k):
        pair_copy(k).wait_recv()
        right, left = lax.rem(x + 1, NX), lax.rem(x + 3, NX)
        across = lax.rem(x + 2, NX)
        own[k, across] = own[k, across] + pair_r[k, across]
        start(k, x_copy, k, 0)
        start(k, x_copy, k, 1)
        own[k, right] = own[k, right] + pair_r[k, right]
        start(k, x_copy, k, 2)
        own[k, left] = own[k, left] + pair_r[k, left]
        start(k, x_copy, k, 3)
        own[k, x] = own[k, x] + pair_r[k, x]

    def e3(k):
        right, left = lax.rem(x + 1, NX), lax.rem(x + 3, NX)
        x_copy(k, 0).wait_recv()
        own[k, right, :, 0:4] = own[k, right, :, 0:4] + xr[k, 0]
        start(k, x_copy, k, 4)
        x_copy(k, 1).wait_recv()
        own[k, left, :, 4:8] = own[k, left, :, 4:8] + xr[k, 1]
        start(k, x_copy, k, 5)

    def e4(k):
        x_copy(k, 3).wait_recv()
        x_copy(k, 4).wait_recv()
        own[k, x, :, 0:4] = own[k, x, :, 0:4] + xf[k, 0] + xf[k, 2]
        x_copy(k, 2).wait_recv()
        x_copy(k, 5).wait_recv()
        own[k, x, :, 4:8] = own[k, x, :, 4:8] + xf[k, 1] + xf[k, 3]
        for d in range(1, NZ):
            start(k, z_copy, k, d)

    def e5(k):
        for d in range(1, NZ):
            z_copy(k, d).wait_recv()
        own[k, x, z] = own[k, x, z] + zr[k, 0] + zr[k, 1] + zr[k, 2]
        for d in range(1, NY):
            start(k, y_copy, k, d)

    def e6(k):
        for d in range(1, NY):
            y_copy(k, d).wait_recv()
        total = own[k, x, z, y]
        for d in range(1, NY):
            total = total + yr[k, d - 1]
        ag[core, y, k] = total

    def step(event, k):
        if k < 2:
            event(k)
        else:
            pl.when(core == 0)(lambda: event(k))

    def hidden_rows(i):
        if i == 0:
            for copy in load_w:
                copy.wait()
        n = rows // 3
        part = pl.ds(i * n, n)
        back = jnp.zeros((n, hidden), F32)
        for u in range(UNITS):
            back = back + lax.dot_general(
                dy_v[u, i * n:(i + 1) * n, :], w_v[u], (((1,), (1,)), ((), ())),
                preferred_element_type=F32,
            )
        alive = lax.broadcasted_iota(jnp.int32, (n, hidden), 0) + i * n < count
        hid_v[i * n:(i + 1) * n, :] = jnp.where(alive, back, jnp.zeros_like(back)).astype(BF16)
        copy = pltpu.make_async_copy(hid_v.at[part], hid_hbm.at[0, part], hid_sem.at[i])
        copy.start()
        return copy

    load_dy[0].wait()
    product(order[0], pair_s.at[0])
    pl.semaphore_wait(barrier, NLINE - 1 + len(offsets))
    start(3, pair_copy, 0)
    load_dy[1].wait()
    product(order[1], own.at[0])
    load_dy[2].wait()
    product(order[2], pair_s.at[1])
    start(3, pair_copy, 1)
    e2(0)
    load_dy[3].wait()
    product(order[3], own.at[1])
    load_dy[4].wait()

    @pl.when(core == 0)
    def _():
        product(2, own.at[2])

    @pl.when(core == 1)
    def _():
        product(2, pair_s.at[2])
        pair_copy(2).start()
        ag[core, y, 2] = jnp.zeros((8, 128), F32)

    e3(0)
    e2(1)
    saved = [hidden_rows(0)]
    e4(0)
    e3(1)
    step(e2, 2)
    saved.append(hidden_rows(1))
    e5(0)
    e4(1)
    step(e3, 2)
    saved.append(hidden_rows(2))
    step(e4, 2)
    e5(1)
    e6(0)
    step(e5, 2)
    e6(1)
    step(e6, 2)

    shard = ag[core, y]
    s1[0] = jnp.sum(jnp.sum(shard * shard, axis=0), axis=0, keepdims=True)
    for i in range(len(offsets)):
        start(3, s1_copy, i)

    for dl in range(1, NLINE):
        start(3, ag_copy, dl)
    for i in range(len(offsets)):
        s1_copy(i).wait_recv()
    s2[0] = jnp.sum(s1[...], axis=0)
    for dl in range(1, NLINE):
        start(3, s2_copy, dl)
    for dl in range(1, NLINE):
        ag_copy(dl).wait_recv()
    for dl in range(1, NLINE):
        s2_copy(dl).wait_recv()
    total = jnp.sum(jnp.sum(s2[...], axis=0), axis=-1, keepdims=True)
    factor = 1.0 / jnp.sqrt(total / entries + 1e-06)
    for u in range(UNITS):
        for q in range(NY):
            r, c = (q % 4) * 8, u * COLS + (q // 4) * 128
            out_ref[0, r:r + 8, c:c + 128] = ag[u // 3, q, u % 3] * factor

    for make, args in sends[0] + sends[1] + sends[3]:
        make(*args).wait_send()

    @pl.when(core == 0)
    def _():
        for make, args in sends[2]:
            make(*args).wait_send()

    @pl.when(core == 1)
    def _():
        pair_copy(2).wait_send()

    for copy in saved:
        copy.wait()


def on_device(act, dy, w_out, counts):
    rows, hidden = act.shape[1:]
    block = w_out.shape[2]
    entries = NM * hidden * block
    dma = pltpu.SemaphoreType.DMA
    tile = (8, 128)
    unit = (NX, NZ, NY) + tile
    scratch = [
        pltpu.VMEM((rows, hidden), BF16),
        pltpu.VMEM((UNITS, rows, COLS), BF16),
        pltpu.VMEM((UNITS, hidden, COLS), BF16),
        pltpu.VMEM((rows, hidden), BF16),
        pltpu.VMEM((hidden, rows), BF16),
        pltpu.VMEM((SLOTS,) + unit, F32),
        pltpu.VMEM((SLOTS,) + unit, F32),
        pltpu.VMEM((SLOTS,) + unit, F32),
        pltpu.VMEM((SLOTS, 2, NZ, 4) + tile, F32),
        pltpu.VMEM((SLOTS, 4, NZ, 4) + tile, F32),
        pltpu.VMEM((SLOTS, NZ - 1, NY) + tile, F32),
        pltpu.VMEM((SLOTS, NY - 1) + tile, F32),
        pltpu.VMEM((2, NY, SLOTS) + tile, F32),
        pltpu.VMEM((NM * NX * NZ, 1, 128), F32),
        pltpu.VMEM((NLINE, 1, 128), F32),
        dma((11,)), dma((3,)),
        dma((SLOTS,)), dma((SLOTS,)),
        dma((SLOTS, 6)), dma((SLOTS, 6)),
        dma((SLOTS, NZ - 1)), dma((SLOTS, NZ - 1)),
        dma((SLOTS, NY - 1)), dma((SLOTS, NY - 1)),
        dma((NLINE - 1,)), dma((NLINE - 1,)),
        dma((NM * NX * NZ - 1,)), dma((NM * NX * NZ - 1,)),
        dma((NLINE - 1,)), dma((NLINE - 1,)),
    ]
    clipped, back = pl.pallas_call(
        functools.partial(kernel, float(entries)),
        out_shape=(
            jax.ShapeDtypeStruct((1, hidden // (NX * NZ), block), F32),
            jax.ShapeDtypeStruct((1, rows, hidden), BF16),
        ),
        in_specs=[
            pl.BlockSpec(memory_space=pltpu.SMEM),
            pl.BlockSpec(memory_space=pl.ANY),
            pl.BlockSpec(memory_space=pl.ANY),
            pl.BlockSpec(memory_space=pl.ANY),
        ],
        out_specs=(pl.BlockSpec(memory_space=pltpu.VMEM), pl.BlockSpec(memory_space=pl.ANY)),
        scratch_shapes=scratch,
        compiler_params=pltpu.CompilerParams(
            collective_id=0, has_side_effects=True, vmem_limit_bytes=48 * 1024 * 1024
        ),
        name="grad_reduce",
    )(counts, act, dy, w_out)
    return clipped, back


def solution(mesh):
    in_specs = (
        P("mod", ("loop", "line"), None),
        P("mod", ("loop", "line"), None),
        P("mod", None, None),
        P("mod", "loop", "line"),
    )
    out_specs = (P("mod", "loop", None), P("mod", ("loop", "line"), None))
    return jax.shard_map(
        on_device, mesh=mesh, in_specs=in_specs, out_specs=out_specs, check_vma=False
    )
```

time: 311 us -> 63.9 us (0.21)
  the two profiles are of different devices: /device:TPU:8 before, /device:TPU:1 now
where the time goes in v1:
time: 63.9 us; the launch traced here: 63.7 us
  Pallas kernels  56.9 us (89%)
  local copies, waits for them, and re-layouts  5.53 us (9%)
  between operations  1.3 us (2%)
    pallas_call x1, Pallas kernels, on_device(): pl.pallas_call(functools.partial(kernel, float(entries)), out_shape=(jax....  56.9 us
    unnamed x8, local copies, waits for them, and re-layouts  5.53 us

profile of v1, /device:TPU:1, one launch (start us, length us, event | category | flops | bytes accessed | tf_op | source)
XLA Modules:
  0.0 63.7 jit_solution(9780114752050311468)
XLA Ops:
  1.3 0.0 copy-start
  1.3 1.5 %copy-done = bf16[1,768,1280]{2,1,0:T(8,128)(2,1)S(1)} copy-done((bf16[1,768,1280]{2,1,0:T(8,128)(2,1)S(1)}, bf16[1,768,1280]{2,1,0:T(8,128)(2,1)}, u32[]{:S(2)}) %copy-start) | copy-done | bytes 1966104
  2.8 0.0 copy-start.1
  2.8 1.3 %copy-done.1 = bf16[1,512,1280]{2,1,0:T(8,128)(2,1)S(1)} copy-done((bf16[1,512,1280]{2,1,0:T(8,128)(2,1)S(1)}, bf16[1,512,1280]{2,1,0:T(8,128)(2,1)}, u32[]{:S(2)}) %copy-start.1) | copy-done | bytes 1310744
  4.1 0.0 copy-start.2
  4.1 1.1 %copy-done.2 = bf16[1,768,512]{2,1,0:T(8,128)(2,1)S(1)} copy-done((bf16[1,768,512]{2,1,0:T(8,128)(2,1)S(1)}, bf16[1,768,512]{2,1,0:T(8,128)(2,1)}, u32[]{:S(2)}) %copy-start.2) | copy-done | bytes 786456
  5.3 56.9 %grad_reduce.1 = (f32[1,32,1280]{2,1,0:T(8,128)S(1)}, bf16[1,768,512]{2,1,0:T(8,128)(2,1)S(1)}) custom-call(s32[1,1,1]{2,1,0:T(1,128)S(6)} %copy.8.cnt_ref, bf16[1,768,512]{2,1,0:T(8,128)(2,1)S(1)} %copy-done.2, bf16[1,768,1280]{2,1,0:T(8,128)(2,1)S(1)} %copy-done, bf16[1,512,1280]{2,1,0:T(8,128)(2,1)S(1)} %copy-done.1), custom_call_target="tpu_custom_call" | custom-call | tf_op jit(solution)/shard_map/grad_reduce/pallas_call | solution.py:318
  62.2 0.7 %copy.9 = f32[1,32,1280]{2,1,0:T(8,128)} copy(f32[1,32,1280]{2,1,0:T(8,128)S(1)} %get-tuple-element.4) | data formatting | bytes 327680
  62.8 0.9 %copy.10 = bf16[1,768,512]{2,1,0:T(8,128)(2,1)} copy(bf16[1,768,512]{2,1,0:T(8,128)(2,1)S(1)} %get-tuple-element.5) | data formatting | bytes 1572864
Async XLA Ops:
  1.3 1.5 %copy-start = (bf16[1,768,1280]{2,1,0:T(8,128)(2,1)S(1)}, bf16[1,768,1280]{2,1,0:T(8,128)(2,1)}, u32[]{:S(2)}) copy-start(bf16[1,768,1280]{2,1,0:T(8,128)(2,1)} %dy_hbm.1) | copy-start | bytes 5898244
  2.8 1.3 %copy-start.1 = (bf16[1,512,1280]{2,1,0:T(8,128)(2,1)S(1)}, bf16[1,512,1280]{2,1,0:T(8,128)(2,1)}, u32[]{:S(2)}) copy-start(bf16[1,512,1280]{2,1,0:T(8,128)(2,1)} %w_hbm.1) | copy-start | bytes 3932164
  4.1 1.1 %copy-start.2 = (bf16[1,768,512]{2,1,0:T(8,128)(2,1)S(1)}, bf16[1,768,512]{2,1,0:T(8,128)(2,1)}, u32[]{:S(2)}) copy-start(bf16[1,768,512]{2,1,0:T(8,128)(2,1)} %act_hbm.1) | copy-start | bytes 2359300

commit v2 on v0

v2 whole, which is shorter than its diff:
```python
import functools

import jax
import jax.numpy as jnp
from jax import lax
from jax.experimental import pallas as pl
from jax.experimental.pallas import tpu as pltpu
from jax.sharding import PartitionSpec as P

MESH = pl.DeviceIdType.MESH
F32 = jnp.float32
BF16 = jnp.bfloat16

NX, NZ, NY, NM = 4, 4, 8, 2
NLINE = NY * 2
COLS = 256
UNITS = ((0, 1, 2), (3, 4))
TILE = (8, 128)


def remote(src, dst, ssem, rsem, peer):
    return pltpu.make_async_remote_copy(
        src_ref=src, dst_ref=dst, send_sem=ssem, recv_sem=rsem, device_id=peer, device_id_type=MESH
    )


def kernel(
    entries,
    cnt, act_hbm, dy_hbm, w_hbm,
    out_ref, hid_ref,
    act_v, dy_v, w_v, act_t,
    pair_s, pair_r, own, xr, xf, zr, yr,
    zr1, xr2, yr1, xr3, zr3,
    ag, s1, s2,
    ld_sem, gossip,
    pair_ss, pair_rs, x_ss, x_rs, z_ss, z_rs, y_ss, y_rs,
    zr1_ss, zr1_rs, xr2_ss, xr2_rs, yr1_ss, yr1_rs, xr3_ss, xr3_rs, zr3_ss, zr3_rs,
    ag_ss, ag_rs, s1_ss, s1_rs, s2_ss, s2_rs,
):
    mod = lax.axis_index("mod")
    loop = lax.axis_index("loop")
    line = lax.axis_index("line")
    x, z = loop // NZ, lax.rem(loop, NZ)
    y, core = line // 2, lax.rem(line, 2)
    rows, hidden = act_v.shape

    def at(dm=0, dx=0, dz=0, dline=0):
        m2 = lax.rem(mod + dm, NM) if dm else mod
        x2 = lax.rem(x + dx, NX) if dx else x
        z2 = lax.rem(z + dz, NZ) if dz else z
        l2 = lax.rem(line + dline, NLINE) if dline else line
        return (m2, x2 * NZ + z2, l2)

    def along_z(d):
        ring = lax.rem(mod * NZ + z + d, NM * NZ)
        return (ring // NZ, x * NZ + lax.rem(ring, NZ), line)

    partner = (mod, loop, y * 2 + (1 - core))
    near_x = [at(dx=1), at(dx=NX - 1)]
    near_yz = [at(dline=2), at(dline=NLINE - 2), along_z(1), along_z(NM * NZ - 1)]

    barrier = pltpu.get_barrier_semaphore()
    for peer in [partner] + near_x + near_yz:
        pl.semaphore_signal(barrier, inc=1, device_id=peer, device_id_type=MESH)

    def tell(r):
        for peer in (near_x + near_yz if r == 0 else near_yz):
            pl.semaphore_signal(gossip.at[r], inc=1, device_id=peer, device_id_type=MESH)

    def hear(r):
        pl.semaphore_wait(gossip.at[r], 6 if r == 0 else 4)

    right, left = lax.rem(x + 1, NX), lax.rem(x + 3, NX)
    across = lax.rem(x + 2, NX)
    lo, hi = pl.ds(0, 4), pl.ds(4, 4)

    def pair_copy(k):
        return remote(pair_s.at[k], pair_r.at[k], pair_ss.at[k], pair_rs.at[k], partner)

    def x_copy(k, i):
        src, dst, dx = (
            (own.at[k, across, :, lo], xr.at[k, 0], 1),
            (own.at[k, across, :, hi], xr.at[k, 1], 3),
            (own.at[k, right, :, hi], xf.at[k, 1], 1),
            (own.at[k, left, :, lo], xf.at[k, 2], 3),
            (own.at[k, right, :, lo], xf.at[k, 0], 1),
            (own.at[k, left, :, hi], xf.at[k, 3], 3),
        )[i]
        return remote(src, dst, x_ss.at[k, i], x_rs.at[k, i], at(dx=dx))

    def z_copy(k, d):
        src = own.at[k, x, lax.rem(z + d, NZ)]
        return remote(src, zr.at[k, d - 1], z_ss.at[k, d - 1], z_rs.at[k, d - 1], at(dz=d))

    def y_copy(k, d):
        src = own.at[k, x, z, lax.rem(y + d, NY)]
        return remote(src, yr.at[k, d - 1], y_ss.at[k, d - 1], y_rs.at[k, d - 1], at(dline=2 * d))

    def zr1_copy(k, d):
        src = own.at[k, :, lax.rem(z + d, NZ)]
        return remote(src, zr1.at[d - 1], zr1_ss.at[d - 1], zr1_rs.at[d - 1], at(dz=d))

    def xr2_copy(k, d):
        src = own.at[k, lax.rem(x + d, NX), z]
        return remote(src, xr2.at[d - 1], xr2_ss.at[d - 1], xr2_rs.at[d - 1], at(dx=d))

    def yr1_copy(k, d):
        src = own.at[k, :, :, lax.rem(y + d, NY)]
        return remote(src, yr1.at[d - 1], yr1_ss.at[d - 1], yr1_rs.at[d - 1], at(dline=2 * d))

    def xr3_copy(k, d):
        src = own.at[k, lax.rem(x + d, NX), :, y]
        return remote(src, xr3.at[d - 1], xr3_ss.at[d - 1], xr3_rs.at[d - 1], at(dx=d))

    def zr3_copy(k, d):
        src = own.at[k, x, lax.rem(z + d, NZ), y]
        return remote(src, zr3.at[d - 1], zr3_ss.at[d - 1], zr3_rs.at[d - 1], at(dz=d))

    def run(c):
        mine, theirs = UNITS[c], UNITS[1 - c]
        sent = []

        def start(make, *args):
            make(*args).start()
            sent.append((make, args))

        def arrive(make, k, n):
            for d in range(1, n):
                make(k, d).wait_recv()

        order = (3, 0, 4, 2, 1) if c == 0 else (0, 3, 2, 4, 1)
        load_act = pltpu.make_async_copy(act_hbm.at[0], act_v, ld_sem.at[0])
        load_act.start()
        load_dy, load_w = {}, []
        for u in order:
            src = dy_hbm.at[0, :, pl.ds(u * COLS, COLS)]
            load_dy[u] = pltpu.make_async_copy(src, dy_v.at[u], ld_sem.at[1 + u])
            load_dy[u].start()
        for u in order:
            src = w_hbm.at[0, :, pl.ds(u * COLS, COLS)]
            load_w.append(pltpu.make_async_copy(src, w_v.at[u], ld_sem.at[6 + u]))
            load_w[-1].start()

        count = cnt[0, 0, 0]
        load_act.wait()
        flipped = act_v[...].T
        alive = lax.broadcasted_iota(jnp.int32, (hidden, rows), 1) < count
        act_t[...] = jnp.where(alive, flipped, jnp.zeros_like(flipped))

        def product(u):
            load_dy[u].wait()
            dst = own.at[mine.index(u)] if u in mine else pair_s.at[theirs.index(u)]
            half = hidden // 2
            for i in range(2):
                acc = jnp.dot(
                    act_t[i * half:(i + 1) * half, :], dy_v[u], preferred_element_type=F32
                )
                tiles = acc.reshape(NX // 2, NZ, 4, 8, COLS)
                dst[2 * i:2 * i + 2, :, 0:4] = tiles[..., 0:128]
                dst[2 * i:2 * i + 2, :, 4:8] = tiles[..., 128:256]

        def hidden_rows(i):
            if i == 0:
                for copy in load_w:
                    copy.wait()
            n = rows // 3
            back = jnp.zeros((n, hidden), F32)
            for u in range(5):
                back = back + lax.dot_general(
                    dy_v[u, i * n:(i + 1) * n, :], w_v[u], (((1,), (1,)), ((), ())),
                    preferred_element_type=F32,
                )
            keep = lax.broadcasted_iota(jnp.int32, (n, hidden), 0) + i * n < count
            hid_ref[0, i * n:(i + 1) * n, :] = jnp.where(keep, back, jnp.zeros_like(back)).astype(BF16)

        def e2(k):
            pair_copy(k).wait_recv()
            own[k, across] = own[k, across] + pair_r[k, across]
            start(x_copy, k, 0)
            start(x_copy, k, 1)
            own[k, right] = own[k, right] + pair_r[k, right]
            start(x_copy, k, 2)
            own[k, left] = own[k, left] + pair_r[k, left]
            start(x_copy, k, 3)
            own[k, x] = own[k, x] + pair_r[k, x]

        def e3(k):
            x_copy(k, 0).wait_recv()
            own[k, right, :, 0:4] = own[k, right, :, 0:4] + xr[k, 0]
            start(x_copy, k, 4)
            x_copy(k, 1).wait_recv()
            own[k, left, :, 4:8] = own[k, left, :, 4:8] + xr[k, 1]
            start(x_copy, k, 5)

        def e4(k):
            x_copy(k, 3).wait_recv()
            x_copy(k, 4).wait_recv()
            own[k, x, :, 0:4] = own[k, x, :, 0:4] + xf[k, 0] + xf[k, 2]
            x_copy(k, 2).wait_recv()
            x_copy(k, 5).wait_recv()
            own[k, x, :, 4:8] = own[k, x, :, 4:8] + xf[k, 1] + xf[k, 3]
            for d in (2, 1, 3):
                start(z_copy, k, d)

        def e5(k):
            arrive(z_copy, k, NZ)
            own[k, x, z] = own[k, x, z] + zr[k, 0] + zr[k, 1] + zr[k, 2]
            for d in (4, 3, 5, 2, 6, 1, 7):
                start(y_copy, k, d)

        def e6(k):
            arrive(y_copy, k, NY)
            total = own[k, x, z, y]
            for d in range(1, NY):
                total = total + yr[k, d - 1]
            ag[c, y, k] = total

        def a1(k):
            pair_copy(k).wait_recv()
            for d in (2, 1, 3, 0):
                to = lax.rem(z + d, NZ)
                own[k, :, to] = own[k, :, to] + pair_r[k, :, to]
                if d:
                    start(zr1_copy, k, d)

        def a2(k):
            arrive(zr1_copy, k, NZ)
            own[k, :, z] = own[k, :, z] + zr1[0] + zr1[1] + zr1[2]
            for d in (2, 1, 3):
                start(xr2_copy, k, d)

        def a3(k):
            arrive(xr2_copy, k, NX)
            own[k, x, z] = own[k, x, z] + xr2[0] + xr2[1] + xr2[2]
            for d in (4, 3, 5, 2, 6, 1, 7):
                start(y_copy, k, d)

        def b1(k):
            pair_copy(k).wait_recv()
            for d in (4, 3, 5, 2, 6, 1, 7, 0):
                to = lax.rem(y + d, NY)
                own[k, :, :, to] = own[k, :, :, to] + pair_r[k, :, :, to]
                if d:
                    start(yr1_copy, k, d)

        def b2(k):
            arrive(yr1_copy, k, NY)
            total = own[k, :, :, y]
            for d in range(1, NY):
                total = total + yr1[d - 1]
            own[k, :, :, y] = total
            for d in (2, 1, 3):
                start(xr3_copy, k, d)

        def b3(k):
            arrive(xr3_copy, k, NX)
            own[k, x, :, y] = own[k, x, :, y] + xr3[0] + xr3[1] + xr3[2]
            for d in (2, 1, 3):
                start(zr3_copy, k, d)

        def b4(k):
            arrive(zr3_copy, k, NZ)
            ag[c, y, k] = own[k, x, z, y] + zr3[0] + zr3[1] + zr3[2]

        product(order[0])
        pl.semaphore_wait(barrier, 7)
        start(pair_copy, 0)
        tell(0)
        product(order[1])
        hear(0)
        tell(1)
        e2(0)
        product(order[2])
        start(pair_copy, 1 if c == 0 else 2)
        hear(1)
        tell(2)
        product(order[3])
        hear(2)
        if c == 0:
            b1(2)
            product(order[4])
            e3(0)
            e2(1)
            hidden_rows(0)
            hidden_rows(1)
            e4(0)
            e3(1)
            hidden_rows(2)
            e4(1)
            e5(0)
            e5(1)
            b2(2)
            e6(0)
            b3(2)
            e6(1)
            b4(2)
        else:
            ag[1, y, 2] = jnp.zeros(TILE, F32)
            a1(1)
            product(order[4])
            start(pair_copy, 1)
            e3(0)
            hidden_rows(0)
            hidden_rows(1)
            e4(0)
            hidden_rows(2)
            e5(0)
            a2(1)
            a3(1)
            e6(0)
            e6(1)
        for make, args in sent:
            make(*args).wait_send()

    pl.when(core == 0)(functools.partial(run, 0))
    pl.when(core == 1)(functools.partial(run, 1))

    offsets = [(dm, dx, dz) for dm in range(NM) for dx in range(NX) for dz in range(NZ)][1:]

    def s1_copy(i):
        return remote(s1.at[0], s1.at[i + 1], s1_ss.at[i], s1_rs.at[i], at(*offsets[i]))

    def s2_copy(d):
        return remote(s2.at[0], s2.at[d], s2_ss.at[d - 1], s2_rs.at[d - 1], at(dline=d))

    def ag_copy(d):
        shard = ag.at[core, y]
        return remote(shard, shard, ag_ss.at[d - 1], ag_rs.at[d - 1], at(dline=d))

    shard = ag[core, y]
    s1[0] = jnp.sum(jnp.sum(shard * shard, axis=0), axis=0, keepdims=True)
    for i in range(len(offsets)):
        s1_copy(i).start()
    for d in range(1, NLINE):
        ag_copy(d).start()
    for i in range(len(offsets)):
        s1_copy(i).wait_recv()
    s2[0] = jnp.sum(s1[...], axis=0)
    for d in range(1, NLINE):
        s2_copy(d).start()
    for d in range(1, NLINE):
        ag_copy(d).wait_recv()
    for i in range(len(offsets)):
        s1_copy(i).wait_send()
    for d in range(1, NLINE):
        ag_copy(d).wait_send()
    for d in range(1, NLINE):
        s2_copy(d).wait_recv()
    total = jnp.sum(jnp.sum(s2[...], axis=0), axis=-1, keepdims=True)
    factor = 1.0 / jnp.sqrt(total / entries + 1e-06)
    for c in range(2):
        for k, u in enumerate(UNITS[c]):
            for q in range(NY):
                r, col = (q % 4) * 8, u * COLS + (q // 4) * 128
                out_ref[0, r:r + 8, col:col + 128] = ag[c, q, k] * factor
    for d in range(1, NLINE):
        s2_copy(d).wait_send()


def store(a_ref, b_ref, a_out, b_out, sem):
    first = pltpu.make_async_copy(b_ref, b_out, sem.at[0])
    second = pltpu.make_async_copy(a_ref, a_out, sem.at[1])
    first.start()
    second.start()
    first.wait()
    second.wait()


def on_device(act, dy, w_out, counts):
    rows, hidden = act.shape[1:]
    block = w_out.shape[2]
    entries = NM * hidden * block
    dma = pltpu.SemaphoreType.DMA
    slots = 3
    unit = (NX, NZ, NY) + TILE
    scratch = [
        pltpu.VMEM((rows, hidden), BF16),
        pltpu.VMEM((5, rows, COLS), BF16),
        pltpu.VMEM((5, hidden, COLS), BF16),
        pltpu.VMEM((hidden, rows), BF16),
        pltpu.VMEM((slots,) + unit, F32),
        pltpu.VMEM((slots,) + unit, F32),
        pltpu.VMEM((slots,) + unit, F32),
        pltpu.VMEM((2, 2, NZ, 4) + TILE, F32),
        pltpu.VMEM((2, 4, NZ, 4) + TILE, F32),
        pltpu.VMEM((2, NZ - 1, NY) + TILE, F32),
        pltpu.VMEM((2, NY - 1) + TILE, F32),
        pltpu.VMEM((NZ - 1, NX, NY) + TILE, F32),
        pltpu.VMEM((NX - 1, NY) + TILE, F32),
        pltpu.VMEM((NY - 1, NX, NZ) + TILE, F32),
        pltpu.VMEM((NX - 1, NZ) + TILE, F32),
        pltpu.VMEM((NZ - 1,) + TILE, F32),
        pltpu.VMEM((2, NY, slots) + TILE, F32),
        pltpu.VMEM((NM * NX * NZ, 1, 128), F32),
        pltpu.VMEM((NLINE, 1, 128), F32),
        dma((11,)), pltpu.SemaphoreType.REGULAR((3,)),
        dma((slots,)), dma((slots,)),
        dma((2, 6)), dma((2, 6)),
        dma((2, NZ - 1)), dma((2, NZ - 1)),
        dma((2, NY - 1)), dma((2, NY - 1)),
        dma((NZ - 1,)), dma((NZ - 1,)),
        dma((NX - 1,)), dma((NX - 1,)),
        dma((NY - 1,)), dma((NY - 1,)),
        dma((NX - 1,)), dma((NX - 1,)),
        dma((NZ - 1,)), dma((NZ - 1,)),
        dma((NLINE - 1,)), dma((NLINE - 1,)),
        dma((NM * NX * NZ - 1,)), dma((NM * NX * NZ - 1,)),
        dma((NLINE - 1,)), dma((NLINE - 1,)),
    ]
    shapes = (
        jax.ShapeDtypeStruct((1, hidden // (NX * NZ), block), F32),
        jax.ShapeDtypeStruct((1, rows, hidden), BF16),
    )
    vmem = pl.BlockSpec(memory_space=pltpu.VMEM)
    anywhere = pl.BlockSpec(memory_space=pl.ANY)
    held = [pltpu.with_memory_space_constraint(v, pltpu.HBM) for v in (act, dy, w_out)]
    clipped, back = pl.pallas_call(
        functools.partial(kernel, float(entries)),
        out_shape=shapes,
        in_specs=[pl.BlockSpec(memory_space=pltpu.SMEM)] + [anywhere] * 3,
        out_specs=(vmem, vmem),
        scratch_shapes=scratch,
        compiler_params=pltpu.CompilerParams(
            collective_id=0, has_side_effects=True, vmem_limit_bytes=48 * 1024 * 1024
        ),
        name="grad_reduce",
    )(counts, *held)
    return pl.pallas_call(
        store,
        out_shape=shapes,
        in_specs=[vmem, vmem],
        out_specs=(anywhere, anywhere),
        scratch_shapes=[dma((2,))],
        name="store",
    )(*[pltpu.with_memory_space_constraint(v, pltpu.VMEM) for v in (clipped, back)])


def solution(mesh):
    in_specs = (
        P("mod", ("loop", "line"), None),
        P("mod", ("loop", "line"), None),
        P("mod", None, None),
        P("mod", "loop", "line"),
    )
    out_specs = (P("mod", "loop", None), P("mod", ("loop", "line"), None))
    return jax.shard_map(
        on_device, mesh=mesh, in_specs=in_specs, out_specs=out_specs, check_vma=False
    )
```

time: 311 us -> 54.2 us (0.17)
  the two profiles are of different devices: /device:TPU:8 before, /device:TPU:1 now
where the time goes in v2:
time: 54.2 us; the launch traced here: 54.1 us
  Pallas kernels  52.8 us (97%)
  between operations  1.28 us (2%)
    pallas_call x1, Pallas kernels, on_device(): pl.pallas_call(functools.partial(kernel, float(entries)), out_shape=shape...  51.9 us

profile of v2, /device:TPU:1, one launch (start us, length us, event | category | flops | bytes accessed | tf_op | source)
XLA Modules:
  0.0 54.1 jit_solution(7102565993934724750)
XLA Ops:
  1.3 51.9 %grad_reduce.1 = (f32[1,32,1280]{2,1,0:T(8,128)S(1)}, bf16[1,768,512]{2,1,0:T(8,128)(2,1)S(1)}) custom-call(s32[1,1,1]{2,1,0:T(1,128)S(6)} %copy.6.cnt, bf16[1,768,512]{2,1,0:T(8,128)(2,1)} %act_hbm.1, bf16[1,768,1280]{2,1,0:T(8,128)(2,1)} %dy_hbm.1, bf16[1,512,1280]{2,1,0:T(8,128)(2,1)} %w_hbm.1), custom_call_target="tpu_custom_call" | custom-call | tf_op jit(solution)/shard_map/grad_reduce/pallas_call | solution.py:417
  53.2 0.9 %store.1 = (f32[1,32,1280]{2,1,0:T(8,128)}, bf16[1,768,512]{2,1,0:T(8,128)(2,1)}) custom-call(f32[1,32,1280]{2,1,0:T(8,128)S(1)} %get-tuple-element.4.a_ref, bf16[1,768,512]{2,1,0:T(8,128)(2,1)S(1)} %get-tuple-element.5.b_ref), custom_call_target="tpu_custom_call" | custom-call | tf_op jit(solution)/shard_map/store/pallas_call | solution.py:428

commit v3 on v2

v3 whole, which is shorter than its diff:
```python
import functools

import jax
import jax.numpy as jnp
from jax import lax
from jax.experimental import pallas as pl
from jax.experimental.pallas import tpu as pltpu
from jax.sharding import PartitionSpec as P

MESH = pl.DeviceIdType.MESH
F32 = jnp.float32
BF16 = jnp.bfloat16

NX, NZ, NY, NM = 4, 4, 8, 2
NLINE = NY * 2
COLS = 256
UNITS = ((0, 1, 2), (3, 4))
TILE = (8, 128)


def remote(src, dst, ssem, rsem, peer):
    return pltpu.make_async_remote_copy(
        src_ref=src, dst_ref=dst, send_sem=ssem, recv_sem=rsem, device_id=peer, device_id_type=MESH
    )


def settle(ref, sem):
    pltpu.make_async_copy(ref, ref, sem).wait()


def kernel(
    entries,
    cnt, act_hbm, dy_hbm, w_hbm,
    out_ref, hid_ref,
    act_v, dy_v, w_v, hid_v, act_t,
    pair_s, pair_r, own, xb, zr, yr,
    zr1, xr2, yrel, yr1, xr3, zr3,
    ag, s1, s2,
    act_sem, dy_sem, w_sem, hid_sem, gossip,
    pair_ss, pair_rs, x_ss, x_rs, z_ss, z_rs, y_ss, y_rs,
    zr1_ss, zr1_rs, xr2_ss, xr2_rs, yrel_ss, yrel_rs, yr1_ss, yr1_rs, xr3_ss, xr3_rs, zr3_ss, zr3_rs,
    ag_ss, ag_rs, s1_ss, s1_rs, s2_ss, s2_rs,
):
    mod = lax.axis_index("mod")
    loop = lax.axis_index("loop")
    line = lax.axis_index("line")
    x, z = loop // NZ, lax.rem(loop, NZ)
    y, core = line // 2, lax.rem(line, 2)
    rows, hidden = act_v.shape
    third = rows // 3

    def at(dm=0, dx=0, dz=0, dline=0):
        m2 = lax.rem(mod + dm, NM) if dm else mod
        x2 = lax.rem(x + dx, NX) if dx else x
        z2 = lax.rem(z + dz, NZ) if dz else z
        l2 = lax.rem(line + dline, NLINE) if dline else line
        return (m2, x2 * NZ + z2, l2)

    def along_z(d):
        ring = lax.rem(mod * NZ + z + d, NM * NZ)
        return (ring // NZ, x * NZ + lax.rem(ring, NZ), line)

    partner = (mod, loop, y * 2 + (1 - core))
    near_x = [at(dx=1), at(dx=NX - 1)]
    near_yz = [at(dline=2), at(dline=NLINE - 2), along_z(1), along_z(NM * NZ - 1)]

    def tell(r):
        for peer in (near_x + near_yz if r == 0 else near_yz):
            pl.semaphore_signal(gossip.at[r], inc=1, device_id=peer, device_id_type=MESH)

    def hear(r):
        pl.semaphore_wait(gossip.at[r], 6 if r == 0 else 4)

    right, left = lax.rem(x + 1, NX), lax.rem(x + 3, NX)
    across = lax.rem(x + 2, NX)
    lo, hi = pl.ds(0, 4), pl.ds(4, 4)

    def send(src, dst, ssem, rsem, peer):
        remote(src, dst, ssem, rsem, peer).start()

    def x_send(k, i):
        src, dx = (
            (own.at[k, across, :, lo], 1),
            (own.at[k, across, :, hi], 3),
            (own.at[k, right, :, hi], 1),
            (own.at[k, left, :, lo], 3),
            (own.at[k, right, :, lo], 1),
            (own.at[k, left, :, hi], 3),
        )[i]
        send(src, xb.at[k, i], x_ss.at[k], x_rs.at[k, min(i, 2)], at(dx=dx))

    def run(c):
        mine, theirs = UNITS[c], UNITS[1 - c]
        finish = []

        order = (3, 0, 4, 2, 1) if c == 0 else (0, 3, 2, 4, 1)
        load_act = []
        for i in range(6):
            part = pl.ds(i * (rows // 6), rows // 6)
            load_act.append(
                pltpu.make_async_copy(act_hbm.at[0, part], act_v.at[part], act_sem.at[i])
            )
            load_act[i].start()
        load_dy = {}
        for u in order:
            src = dy_hbm.at[0, :, pl.ds(u * COLS, COLS)]
            load_dy[u] = pltpu.make_async_copy(src, dy_v.at[u], dy_sem.at[u])
            load_dy[u].start()

        barrier = pltpu.get_barrier_semaphore()
        for peer in [partner] + near_x + near_yz:
            pl.semaphore_signal(barrier, inc=1, device_id=peer, device_id_type=MESH)

        count = cnt[0, 0, 0]
        for i in range(3):
            load_act[2 * i].wait()
            load_act[2 * i + 1].wait()
            flipped = act_v[i * third:(i + 1) * third, :].T
            alive = lax.broadcasted_iota(jnp.int32, (hidden, third), 1) + i * third < count
            act_t[:, i * third:(i + 1) * third] = jnp.where(alive, flipped, jnp.zeros_like(flipped))

        def product(u):
            load_dy[u].wait()
            dst = own.at[mine.index(u)] if u in mine else pair_s.at[theirs.index(u)]
            half = hidden // 2
            for i in range(2):
                acc = jnp.dot(
                    act_t[i * half:(i + 1) * half, :], dy_v[u], preferred_element_type=F32
                )
                tiles = acc.reshape(NX // 2, NZ, 4, 8, COLS)
                dst[2 * i:2 * i + 2, :, 0:4] = tiles[..., 0:128]
                dst[2 * i:2 * i + 2, :, 4:8] = tiles[..., 128:256]

        def send_pair(k):
            if theirs[k] in (2, 4):
                send(pair_s.at[k], pair_r.at[k], pair_ss.at[k], pair_rs.at[k, 0], partner)
            else:
                for d in (2, 1, 3, 0):
                    to = lax.rem(x + d, NX)
                    send(pair_s.at[k, to], pair_r.at[k, to], pair_ss.at[k], pair_rs.at[k, d], partner)
            finish.append((pair_s.at[k], pair_ss.at[k]))

        def hidden_rows(i):
            if i == 0:
                settle(w_v, w_sem)
            back = jnp.zeros((third, hidden), F32)
            for u in range(5):
                back = back + lax.dot_general(
                    dy_v[u, i * third:(i + 1) * third, :], w_v[u], (((1,), (1,)), ((), ())),
                    preferred_element_type=F32,
                )
            keep = lax.broadcasted_iota(jnp.int32, (third, hidden), 0) + i * third < count
            back = jnp.where(keep, back, jnp.zeros_like(back))
            hid_v[i * third:(i + 1) * third, :] = back.astype(BF16)
            part = pl.ds(i * third, third)
            pltpu.make_async_copy(hid_v.at[part], hid_ref.at[0, part], hid_sem).start()

        def merge_x(k, d):
            to = lax.rem(x + d, NX)
            settle(pair_r.at[k, to], pair_rs.at[k, d])
            own[k, to] = own[k, to] + pair_r[k, to]

        def e2(k):
            merge_x(k, 2)
            x_send(k, 0)
            x_send(k, 1)
            merge_x(k, 1)
            x_send(k, 2)
            merge_x(k, 3)
            x_send(k, 3)
            merge_x(k, 0)

        def e3(k):
            settle(xb.at[k, 0], x_rs.at[k, 0])
            own[k, right, :, 0:4] = own[k, right, :, 0:4] + xb[k, 0]
            x_send(k, 4)
            settle(xb.at[k, 1], x_rs.at[k, 1])
            own[k, left, :, 4:8] = own[k, left, :, 4:8] + xb[k, 1]
            x_send(k, 5)
            finish.append((xb.at[k], x_ss.at[k]))

        def e4(k):
            settle(xb.at[k, pl.ds(2, 4)], x_rs.at[k, 2])
            own[k, x, :, 0:4] = own[k, x, :, 0:4] + xb[k, 3] + xb[k, 4]
            own[k, x, :, 4:8] = own[k, x, :, 4:8] + xb[k, 2] + xb[k, 5]
            for d in (2, 1, 3):
                src = own.at[k, x, lax.rem(z + d, NZ)]
                send(src, zr.at[k, d - 1], z_ss.at[k], z_rs.at[k], at(dz=d))
            finish.append((zr.at[k], z_ss.at[k]))

        def to_y(k):
            for d in (4, 3, 5, 2, 6, 1, 7):
                src = own.at[k, x, z, lax.rem(y + d, NY)]
                send(src, yr.at[k, d - 1], y_ss.at[k], y_rs.at[k], at(dline=2 * d))
            finish.append((yr.at[k], y_ss.at[k]))

        def e5(k):
            settle(zr.at[k], z_rs.at[k])
            own[k, x, z] = own[k, x, z] + zr[k, 0] + zr[k, 1] + zr[k, 2]
            to_y(k)

        def e6(k):
            settle(yr.at[k], y_rs.at[k])
            total = own[k, x, z, y]
            for d in range(1, NY):
                total = total + yr[k, d - 1]
            ag[line, k] = total

        def a1(k):
            settle(pair_r.at[k], pair_rs.at[k, 0])
            for d in (2, 1, 3, 0):
                to = lax.rem(z + d, NZ)
                own[k, :, to] = own[k, :, to] + pair_r[k, :, to]
                if d:
                    send(own.at[k, :, to], zr1.at[d - 1], zr1_ss.at[0], zr1_rs.at[0], at(dz=d))
            finish.append((zr1, zr1_ss.at[0]))

        def a2(k):
            settle(zr1, zr1_rs.at[0])
            own[k, :, z] = own[k, :, z] + zr1[0] + zr1[1] + zr1[2]
            for d in (2, 1, 3):
                src = own.at[k, lax.rem(x + d, NX), z]
                send(src, xr2.at[d - 1], xr2_ss.at[0], xr2_rs.at[0], at(dx=d))
            finish.append((xr2, xr2_ss.at[0]))

        def a3(k):
            settle(xr2, xr2_rs.at[0])
            own[k, x, z] = own[k, x, z] + xr2[0] + xr2[1] + xr2[2]
            to_y(k)

        slot_of = {3: 0, 2: 1, 6: 2, 1: 3, 7: 4, 5: 5}

        def y_send(k, d):
            src = own.at[k, :, :, lax.rem(y + d, NY)]
            send(src, yr1.at[slot_of[d]], yr1_ss.at[0], yr1_rs.at[0], at(dline=2 * d))

        def b1(k):
            settle(pair_r.at[k], pair_rs.at[k, 0])
            for d in (4, 3, 2, 6, 1, 7, 5, 0):
                to = lax.rem(y + d, NY)
                own[k, :, :, to] = own[k, :, :, to] + pair_r[k, :, :, to]
                if d == 4:
                    send(own.at[k, :, :, to], yrel, yrel_ss.at[0], yrel_rs.at[0], at(dline=NLINE - 2))
                elif d in (3, 2, 6, 1, 7):
                    y_send(k, d)
            finish.append((yrel, yrel_ss.at[0]))

        def relay_y(k):
            settle(yrel, yrel_rs.at[0])
            to = lax.rem(y + 5, NY)
            own[k, :, :, to] = own[k, :, :, to] + yrel[...]
            y_send(k, 5)
            finish.append((yr1, yr1_ss.at[0]))

        def b2(k):
            settle(yr1, yr1_rs.at[0])
            total = own[k, :, :, y]
            for i in range(6):
                total = total + yr1[i]
            own[k, :, :, y] = total
            for d in (2, 1, 3):
                src = own.at[k, lax.rem(x + d, NX), :, y]
                send(src, xr3.at[d - 1], xr3_ss.at[0], xr3_rs.at[0], at(dx=d))
            finish.append((xr3, xr3_ss.at[0]))

        def b3(k):
            settle(xr3, xr3_rs.at[0])
            own[k, x, :, y] = own[k, x, :, y] + xr3[0] + xr3[1] + xr3[2]
            for d in (2, 1, 3):
                src = own.at[k, x, lax.rem(z + d, NZ), y]
                send(src, zr3.at[d - 1], zr3_ss.at[0], zr3_rs.at[0], at(dz=d))
            finish.append((zr3, zr3_ss.at[0]))

        def b4(k):
            settle(zr3, zr3_rs.at[0])
            ag[line, k] = own[k, x, z, y] + zr3[0] + zr3[1] + zr3[2]

        product(order[0])
        pl.semaphore_wait(barrier, 7)
        tell(0)
        send_pair(0)
        for u in range(5):
            src = w_hbm.at[0, :, pl.ds(u * COLS, COLS)]
            pltpu.make_async_copy(src, w_v.at[u], w_sem).start()
        product(order[1])
        product(order[2])
        send_pair(1 if c == 0 else 2)
        hear(0)
        tell(1)
        e2(0)
        product(order[3])
        product(order[4])
        if c == 1:
            send_pair(1)
        hear(1)
        tell(2)
        if c == 0:
            b1(2)
            e2(1)
            e3(0)
            hidden_rows(0)
            relay_y(2)
            e3(1)
            hidden_rows(1)
            hear(2)
            e4(0)
            hidden_rows(2)
            e4(1)
            e5(0)
            b2(2)
            e5(1)
            b3(2)
            e6(0)
            e6(1)
            b4(2)
        else:
            ag[line, 2] = jnp.zeros(TILE, F32)
            a1(1)
            e3(0)
            hidden_rows(0)
            hidden_rows(1)
            hear(2)
            hidden_rows(2)
            e4(0)
            a2(1)
            e5(0)
            a3(1)
            e6(0)
            e6(1)
        for ref, sem in finish:
            settle(ref, sem)
        settle(hid_v, hid_sem)

    pl.when(core == 0)(functools.partial(run, 0))
    pl.when(core == 1)(functools.partial(run, 1))

    offsets = [(dm, dx, dz) for dm in range(NM) for dx in range(NX) for dz in range(NZ)][1:]
    shard = ag[line]
    s1[0] = jnp.sum(jnp.sum(shard * shard, axis=0), axis=0, keepdims=True)
    for i, offset in enumerate(offsets):
        send(s1.at[0], s1.at[i + 1], s1_ss.at[0], s1_rs.at[0], at(*offset))
    for d in range(1, NLINE):
        send(ag.at[line], ag.at[line], ag_ss.at[0], ag_rs.at[0], at(dline=d))
    rest1, rest2, rest3 = s1.at[pl.ds(1, len(offsets))], s2.at[pl.ds(1, NLINE - 1)], ag.at[pl.ds(0, NLINE - 1)]
    settle(rest1, s1_rs.at[0])
    s2[0] = jnp.sum(s1[...], axis=0)
    for d in range(1, NLINE):
        send(s2.at[0], s2.at[d], s2_ss.at[0], s2_rs.at[0], at(dline=d))
    settle(rest1, s1_ss.at[0])
    settle(rest3, ag_rs.at[0])
    settle(rest3, ag_ss.at[0])
    settle(rest2, s2_rs.at[0])
    total = jnp.sum(jnp.sum(s2[...], axis=0), axis=-1, keepdims=True)
    factor = 1.0 / jnp.sqrt(total / entries + 1e-06)
    for c in range(2):
        for k, u in enumerate(UNITS[c]):
            for q in range(NY):
                r, col = (q % 4) * 8, u * COLS + (q // 4) * 128
                out_ref[0, r:r + 8, col:col + 128] = ag[q * 2 + c, k] * factor
    settle(rest2, s2_ss.at[0])


def store(a_ref, b_ref, a_out, b_out, sem):
    n = b_ref.shape[1] // 8
    copies = [pltpu.make_async_copy(a_ref, a_out, sem.at[8])]
    for i in range(8):
        part = pl.ds(i * n, n)
        copies.append(pltpu.make_async_copy(b_ref.at[0, part], b_out.at[0, part], sem.at[i]))
    for copy in copies:
        copy.start()
    for copy in copies:
        copy.wait()


def on_device(act, dy, w_out, counts):
    rows, hidden = act.shape[1:]
    block = w_out.shape[2]
    entries = NM * hidden * block
    dma = pltpu.SemaphoreType.DMA
    slots = 3
    unit = (NX, NZ, NY) + TILE
    scratch = [
        pltpu.VMEM((rows, hidden), BF16),
        pltpu.VMEM((5, rows, COLS), BF16),
        pltpu.VMEM((5, hidden, COLS), BF16),
        pltpu.VMEM((rows, hidden), BF16),
        pltpu.VMEM((hidden, rows), BF16),
        pltpu.VMEM((slots,) + unit, F32),
        pltpu.VMEM((slots,) + unit, F32),
        pltpu.VMEM((slots,) + unit, F32),
        pltpu.VMEM((2, 6, NZ, 4) + TILE, F32),
        pltpu.VMEM((2, NZ - 1, NY) + TILE, F32),
        pltpu.VMEM((2, NY - 1) + TILE, F32),
        pltpu.VMEM((NZ - 1, NX, NY) + TILE, F32),
        pltpu.VMEM((NX - 1, NY) + TILE, F32),
        pltpu.VMEM((NX, NZ) + TILE, F32),
        pltpu.VMEM((NY - 2, NX, NZ) + TILE, F32),
        pltpu.VMEM((NX - 1, NZ) + TILE, F32),
        pltpu.VMEM((NZ - 1,) + TILE, F32),
        pltpu.VMEM((NLINE, slots) + TILE, F32),
        pltpu.VMEM((NM * NX * NZ, 1, 128), F32),
        pltpu.VMEM((NLINE, 1, 128), F32),
        dma((6,)), dma((5,)), dma(()), dma(()), pltpu.SemaphoreType.REGULAR((3,)),
        dma((slots,)), dma((slots, 4)),
        dma((2,)), dma((2, 3)),
        dma((2,)), dma((2,)), dma((2,)), dma((2,)),
    ] + [dma((1,))] * 18
    shapes = (
        jax.ShapeDtypeStruct((1, hidden // (NX * NZ), block), F32),
        jax.ShapeDtypeStruct((1, rows, hidden), BF16),
    )
    vmem = pl.BlockSpec(memory_space=pltpu.VMEM)
    anywhere = pl.BlockSpec(memory_space=pl.ANY)
    held = [pltpu.with_memory_space_constraint(v, pltpu.HBM) for v in (act, dy, w_out)]
    clipped, back = pl.pallas_call(
        functools.partial(kernel, float(entries)),
        out_shape=shapes,
        in_specs=[pl.BlockSpec(memory_space=pltpu.SMEM)] + [anywhere] * 3,
        out_specs=(vmem, anywhere),
        scratch_shapes=scratch,
        compiler_params=pltpu.CompilerParams(
            collective_id=0, has_side_effects=True, vmem_limit_bytes=48 * 1024 * 1024
        ),
        name="grad_reduce",
    )(counts, *held)
    return pl.pallas_call(
        store,
        out_shape=shapes,
        in_specs=[vmem, vmem],
        out_specs=(anywhere, anywhere),
        scratch_shapes=[dma((9,))],
        name="store",
    )(*[pltpu.with_memory_space_constraint(v, pltpu.VMEM) for v in (clipped, back)])


def solution(mesh):
    in_specs = (
        P("mod", ("loop", "line"), None),
        P("mod", ("loop", "line"), None),
        P("mod", None, None),
        P("mod", "loop", "line"),
    )
    out_specs = (P("mod", "loop", None), P("mod", ("loop", "line"), None))
    return jax.shard_map(
        on_device, mesh=mesh, in_specs=in_specs, out_specs=out_specs, check_vma=False
    )
```

time: 54.2 us -> 48.6 us (0.90)
  Pallas kernels: 52.8 us -> 47.2 us
    pallas_call x1, Pallas kernels: 51.9 us -> 46.2 us  [on_device(): pl.pallas_call(functools.partial(kernel, float(entries)), out_shape=shape...]
where the time goes in v3:
time: 48.6 us; the launch traced here: 48.4 us
  Pallas kernels  47.2 us (97%)
  between operations  1.28 us (3%)
    pallas_call x1, Pallas kernels, on_device(): pl.pallas_call(functools.partial(kernel, float(entries)), out_shape=shape...  46.2 us
    pallas_call x1, Pallas kernels, on_device(): pl.pallas_call(store, out_shape=shapes, in_specs=[vmem, vmem], out_specs=...  1 us

profile of v3, /device:TPU:1, one launch (start us, length us, event | category | flops | bytes accessed | tf_op | source)
XLA Modules:
  0.0 48.4 jit_solution(15807533543816638136)
XLA Ops:
  1.3 46.2 %grad_reduce.1 = (f32[1,32,1280]{2,1,0:T(8,128)S(1)}, bf16[1,768,512]{2,1,0:T(8,128)(2,1)S(1)}) custom-call(s32[1,1,1]{2,1,0:T(1,128)S(6)} %copy.6.cnt, bf16[1,768,512]{2,1,0:T(8,128)(2,1)} %act_hbm.1, bf16[1,768,1280]{2,1,0:T(8,128)(2,1)} %dy_hbm.1, bf16[1,512,1280]{2,1,0:T(8,128)(2,1)} %w_hbm.1), custom_call_target="tpu_custom_call" | custom-call | tf_op jit(solution)/shard_map/grad_reduce/pallas_call | solution.py:415
  47.4 1.0 %store.1 = (f32[1,32,1280]{2,1,0:T(8,128)}, bf16[1,768,512]{2,1,0:T(8,128)(2,1)}) custom-call(f32[1,32,1280]{2,1,0:T(8,128)S(1)} %get-tuple-element.4.a_ref, bf16[1,768,512]{2,1,0:T(8,128)(2,1)S(1)} %get-tuple-element.5.b_ref), custom_call_target="tpu_custom_call" | custom-call | tf_op jit(solution)/shard_map/store/pallas_call | solution.py:426

commit v4 on v3

--- a/solution.py
+++ b/solution.py
@@ -16,6 +16,7 @@
 COLS = 256
 UNITS = ((0, 1, 2), (3, 4))
 TILE = (8, 128)
+Y_THEN_Z = (0, 1)
 
 
 def remote(src, dst, ssem, rsem, peer):
@@ -33,11 +34,11 @@
     cnt, act_hbm, dy_hbm, w_hbm,
     out_ref, hid_ref,
     act_v, dy_v, w_v, hid_v, act_t,
-    pair_s, pair_r, own, xb, zr, yr,
+    pair_s, pair_r, own, xb, zr, yz, yzz, yr,
     zr1, xr2, yrel, yr1, xr3, zr3,
     ag, s1, s2,
     act_sem, dy_sem, w_sem, hid_sem, gossip,
-    pair_ss, pair_rs, x_ss, x_rs, z_ss, z_rs, y_ss, y_rs,
+    pair_ss, pair_rs, x_ss, x_rs, z_ss, z_rs, yz_ss, yz_rs, y_ss, y_rs,
     zr1_ss, zr1_rs, xr2_ss, xr2_rs, yrel_ss, yrel_rs, yr1_ss, yr1_rs, xr3_ss, xr3_rs, zr3_ss, zr3_rs,
     ag_ss, ag_rs, s1_ss, s1_rs, s2_ss, s2_rs,
 ):
@@ -88,6 +89,21 @@
             (own.at[k, left, :, hi], 3),
         )[i]
         send(src, xb.at[k, i], x_ss.at[k], x_rs.at[k, min(i, 2)], at(dx=dx))
+
+    count = cnt[0, 0, 0]
+
+    def hidden_rows(i):
+        back = jnp.zeros((third, hidden), F32)
+        for u in range(5):
+            back = back + lax.dot_general(
+                dy_v[u, i * third:(i + 1) * third, :], w_v[u], (((1,), (1,)), ((), ())),
+                preferred_element_type=F32,
+            )
+        keep = lax.broadcasted_iota(jnp.int32, (third, hidden), 0) + i * third < count
+        back = jnp.where(keep, back, jnp.zeros_like(back))
+        hid_v[i * third:(i + 1) * third, :] = back.astype(BF16)
+        part = pl.ds(i * third, third)
+        pltpu.make_async_copy(hid_v.at[part], hid_ref.at[0, part], hid_sem).start()
 
     def run(c):
         mine, theirs = UNITS[c], UNITS[1 - c]
@@ -105,19 +121,22 @@
         for u in order:
             src = dy_hbm.at[0, :, pl.ds(u * COLS, COLS)]
             load_dy[u] = pltpu.make_async_copy(src, dy_v.at[u], dy_sem.at[u])
-            load_dy[u].start()
+        load_dy[order[0]].start()
+        load_dy[order[1]].start()
 
         barrier = pltpu.get_barrier_semaphore()
         for peer in [partner] + near_x + near_yz:
             pl.semaphore_signal(barrier, inc=1, device_id=peer, device_id_type=MESH)
 
-        count = cnt[0, 0, 0]
         for i in range(3):
             load_act[2 * i].wait()
             load_act[2 * i + 1].wait()
             flipped = act_v[i * third:(i + 1) * third, :].T
             alive = lax.broadcasted_iota(jnp.int32, (hidden, third), 1) + i * third < count
             act_t[:, i * third:(i + 1) * third] = jnp.where(alive, flipped, jnp.zeros_like(flipped))
+
+        for u in order[2:]:
+            load_dy[u].start()
 
         def product(u):
             load_dy[u].wait()
@@ -131,29 +150,18 @@
                 dst[2 * i:2 * i + 2, :, 0:4] = tiles[..., 0:128]
                 dst[2 * i:2 * i + 2, :, 4:8] = tiles[..., 128:256]
 
+        late = 1 if c == 0 else 2
+
         def send_pair(k):
             if theirs[k] in (2, 4):
                 send(pair_s.at[k], pair_r.at[k], pair_ss.at[k], pair_rs.at[k, 0], partner)
             else:
-                for d in (2, 1, 3, 0):
+                for d in (2, 1, 3) if k == 0 else (2, 1, 3, 0):
                     to = lax.rem(x + d, NX)
                     send(pair_s.at[k, to], pair_r.at[k, to], pair_ss.at[k], pair_rs.at[k, d], partner)
+            if k == late:
+                send(pair_s.at[0, x], pair_r.at[0, x], pair_ss.at[0], pair_rs.at[0, 0], partner)
             finish.append((pair_s.at[k], pair_ss.at[k]))
-
-        def hidden_rows(i):
-            if i == 0:
-                settle(w_v, w_sem)
-            back = jnp.zeros((third, hidden), F32)
-            for u in range(5):
-                back = back + lax.dot_general(
-                    dy_v[u, i * third:(i + 1) * third, :], w_v[u], (((1,), (1,)), ((), ())),
-                    preferred_element_type=F32,
-                )
-            keep = lax.broadcasted_iota(jnp.int32, (third, hidden), 0) + i * third < count
-            back = jnp.where(keep, back, jnp.zeros_like(back))
-            hid_v[i * third:(i + 1) * third, :] = back.astype(BF16)
-            part = pl.ds(i * third, third)
-            pltpu.make_async_copy(hid_v.at[part], hid_ref.at[0, part], hid_sem).start()
 
         def merge_x(k, d):
             to = lax.rem(x + d, NX)
@@ -168,7 +176,6 @@
             x_send(k, 2)
             merge_x(k, 3)
             x_send(k, 3)
-            merge_x(k, 0)
 
         def e3(k):
             settle(xb.at[k, 0], x_rs.at[k, 0])
@@ -180,9 +187,16 @@
             finish.append((xb.at[k], x_ss.at[k]))
 
         def e4(k):
+            merge_x(k, 0)
             settle(xb.at[k, pl.ds(2, 4)], x_rs.at[k, 2])
             own[k, x, :, 0:4] = own[k, x, :, 0:4] + xb[k, 3] + xb[k, 4]
             own[k, x, :, 4:8] = own[k, x, :, 4:8] + xb[k, 2] + xb[k, 5]
+            if k in Y_THEN_Z:
+                for d in (4, 3, 5, 2, 6, 1, 7):
+                    src = own.at[k, x, :, lax.rem(y + d, NY)]
+                    send(src, yz.at[k, d - 1], yz_ss.at[k], yz_rs.at[k], at(dline=2 * d))
+                finish.append((yz.at[k], yz_ss.at[k]))
+                return
             for d in (2, 1, 3):
                 src = own.at[k, x, lax.rem(z + d, NZ)]
                 send(src, zr.at[k, d - 1], z_ss.at[k], z_rs.at[k], at(dz=d))
@@ -195,11 +209,26 @@
             finish.append((yr.at[k], y_ss.at[k]))
 
         def e5(k):
+            if k in Y_THEN_Z:
+                settle(yz.at[k], yz_rs.at[k])
+                total = own[k, x, :, y]
+                for d in range(1, NY):
+                    total = total + yz[k, d - 1]
+                own[k, x, :, y] = total
+                for d in (2, 1, 3):
+                    src = own.at[k, x, lax.rem(z + d, NZ), y]
+                    send(src, yzz.at[k, d - 1], z_ss.at[k], z_rs.at[k], at(dz=d))
+                finish.append((yzz.at[k], z_ss.at[k]))
+                return
             settle(zr.at[k], z_rs.at[k])
             own[k, x, z] = own[k, x, z] + zr[k, 0] + zr[k, 1] + zr[k, 2]
             to_y(k)
 
         def e6(k):
+            if k in Y_THEN_Z and (c, k) != (1, 1):
+                settle(yzz.at[k], z_rs.at[k])
+                ag[line, k] = own[k, x, z, y] + yzz[k, 0] + yzz[k, 1] + yzz[k, 2]
+                return
             settle(yr.at[k], y_rs.at[k])
             total = own[k, x, z, y]
             for d in range(1, NY):
@@ -236,12 +265,12 @@
 
         def b1(k):
             settle(pair_r.at[k], pair_rs.at[k, 0])
-            for d in (4, 3, 2, 6, 1, 7, 5, 0):
+            for d in (4, 2, 6, 1, 7, 3, 5, 0):
                 to = lax.rem(y + d, NY)
                 own[k, :, :, to] = own[k, :, :, to] + pair_r[k, :, :, to]
                 if d == 4:
                     send(own.at[k, :, :, to], yrel, yrel_ss.at[0], yrel_rs.at[0], at(dline=NLINE - 2))
-                elif d in (3, 2, 6, 1, 7):
+                elif d in (2, 6, 1, 7):
                     y_send(k, d)
             finish.append((yrel, yrel_ss.at[0]))
 
@@ -285,42 +314,38 @@
         product(order[1])
         product(order[2])
         send_pair(1 if c == 0 else 2)
+        e2(0)
         hear(0)
         tell(1)
-        e2(0)
         product(order[3])
         product(order[4])
-        if c == 1:
+        if c == 0:
+            b1(2)
+            e2(1)
+        else:
             send_pair(1)
         hear(1)
         tell(2)
         if c == 0:
-            b1(2)
-            e2(1)
+            y_send(2, 3)
             e3(0)
-            hidden_rows(0)
             relay_y(2)
             e3(1)
-            hidden_rows(1)
             hear(2)
             e4(0)
-            hidden_rows(2)
             e4(1)
+            b2(2)
             e5(0)
-            b2(2)
+            b3(2)
             e5(1)
-            b3(2)
+            b4(2)
             e6(0)
             e6(1)
-            b4(2)
         else:
             ag[line, 2] = jnp.zeros(TILE, F32)
             a1(1)
             e3(0)
-            hidden_rows(0)
-            hidden_rows(1)
             hear(2)
-            hidden_rows(2)
             e4(0)
             a2(1)
             e5(0)
@@ -329,12 +354,11 @@
             e6(1)
         for ref, sem in finish:
             settle(ref, sem)
-        settle(hid_v, hid_sem)
 
     pl.when(core == 0)(functools.partial(run, 0))
     pl.when(core == 1)(functools.partial(run, 1))
 
-    offsets = [(dm, dx, dz) for dm in range(NM) for dx in range(NX) for dz in range(NZ)][1:]
+    offsets = [(dm, dx, dz) for dm in range(NM) for dx in range(NX) for dz in range(NZ)][:0:-1]
     shard = ag[line]
     s1[0] = jnp.sum(jnp.sum(shard * shard, axis=0), axis=0, keepdims=True)
     for i, offset in enumerate(offsets):
@@ -342,6 +366,9 @@
     for d in range(1, NLINE):
         send(ag.at[line], ag.at[line], ag_ss.at[0], ag_rs.at[0], at(dline=d))
     rest1, rest2, rest3 = s1.at[pl.ds(1, len(offsets))], s2.at[pl.ds(1, NLINE - 1)], ag.at[pl.ds(0, NLINE - 1)]
+    settle(w_v, w_sem)
+    for i in range(3):
+        hidden_rows(i)
     settle(rest1, s1_rs.at[0])
     s2[0] = jnp.sum(s1[...], axis=0)
     for d in range(1, NLINE):
@@ -358,12 +385,13 @@
                 r, col = (q % 4) * 8, u * COLS + (q // 4) * 128
                 out_ref[0, r:r + 8, col:col + 128] = ag[q * 2 + c, k] * factor
     settle(rest2, s2_ss.at[0])
+    settle(hid_v, hid_sem)
 
 
 def store(a_ref, b_ref, a_out, b_out, sem):
-    n = b_ref.shape[1] // 8
-    copies = [pltpu.make_async_copy(a_ref, a_out, sem.at[8])]
-    for i in range(8):
+    n = b_ref.shape[1] // 2
+    copies = [pltpu.make_async_copy(a_ref, a_out, sem.at[2])]
+    for i in range(2):
         part = pl.ds(i * n, n)
         copies.append(pltpu.make_async_copy(b_ref.at[0, part], b_out.at[0, part], sem.at[i]))
     for copy in copies:
@@ -390,6 +418,8 @@
         pltpu.VMEM((slots,) + unit, F32),
         pltpu.VMEM((2, 6, NZ, 4) + TILE, F32),
         pltpu.VMEM((2, NZ - 1, NY) + TILE, F32),
+        pltpu.VMEM((2, NY - 1, NZ) + TILE, F32),
+        pltpu.VMEM((2, NZ - 1) + TILE, F32),
         pltpu.VMEM((2, NY - 1) + TILE, F32),
         pltpu.VMEM((NZ - 1, NX, NY) + TILE, F32),
         pltpu.VMEM((NX - 1, NY) + TILE, F32),
@@ -403,7 +433,7 @@
         dma((6,)), dma((5,)), dma(()), dma(()), pltpu.SemaphoreType.REGULAR((3,)),
         dma((slots,)), dma((slots, 4)),
         dma((2,)), dma((2, 3)),
-        dma((2,)), dma((2,)), dma((2,)), dma((2,)),
+        dma((2,)), dma((2,)), dma((2,)), dma((2,)), dma((2,)), dma((2,)),
     ] + [dma((1,))] * 18
     shapes = (
         jax.ShapeDtypeStruct((1, hidden // (NX * NZ), block), F32),
@@ -428,7 +458,7 @@
         out_shape=shapes,
         in_specs=[vmem, vmem],
         out_specs=(anywhere, anywhere),
-        scratch_shapes=[dma((9,))],
+        scratch_shapes=[dma((3,))],
         name="store",
     )(*[pltpu.with_memory_space_constraint(v, pltpu.VMEM) for v in (clipped, back)])
 

time: 48.6 us -> 47.9 us (0.986)
  Pallas kernels: 47.2 us -> 46.5 us
    pallas_call x1, Pallas kernels: 46.2 us -> 45.5 us  [on_device(): pl.pallas_call(functools.partial(kernel, float(entries)), out_shape=shape...]
where the time goes in v4:
time: 47.9 us; the launch traced here: 47.8 us
  Pallas kernels  46.5 us (97%)
  between operations  1.28 us (3%)
    pallas_call x1, Pallas kernels, on_device(): pl.pallas_call(functools.partial(kernel, float(entries)), out_shape=shape...  45.5 us

profile of v4, /device:TPU:1, one launch (start us, length us, event | category | flops | bytes accessed | tf_op | source)
XLA Modules:
  0.0 47.8 jit_solution(18047974823145164286)
XLA Ops:
  1.3 45.5 %grad_reduce.1 = (f32[1,32,1280]{2,1,0:T(8,128)S(1)}, bf16[1,768,512]{2,1,0:T(8,128)(2,1)S(1)}) custom-call(s32[1,1,1]{2,1,0:T(1,128)S(6)} %copy.6.cnt, bf16[1,768,512]{2,1,0:T(8,128)(2,1)} %act_hbm.1, bf16[1,768,1280]{2,1,0:T(8,128)(2,1)} %dy_hbm.1, bf16[1,512,1280]{2,1,0:T(8,128)(2,1)} %w_hbm.1), custom_call_target="tpu_custom_call" | custom-call | tf_op jit(solution)/shard_map/grad_reduce/pallas_call | solution.py:445
  46.8 1.0 %store.1 = (f32[1,32,1280]{2,1,0:T(8,128)}, bf16[1,768,512]{2,1,0:T(8,128)(2,1)}) custom-call(f32[1,32,1280]{2,1,0:T(8,128)S(1)} %get-tuple-element.4.a_ref, bf16[1,768,512]{2,1,0:T(8,128)(2,1)S(1)} %get-tuple-element.5.b_ref), custom_call_target="tpu_custom_call" | custom-call | tf_op jit(solution)/shard_map/store/pallas_call | solution.py:456

commit v5 on v4

--- a/solution.py
+++ b/solution.py
@@ -16,7 +16,7 @@
 COLS = 256
 UNITS = ((0, 1, 2), (3, 4))
 TILE = (8, 128)
-Y_THEN_Z = (0, 1)
+Y_THEN_Z = ((1, 0), (0, 1))
 
 
 def remote(src, dst, ssem, rsem, peer):
@@ -191,7 +191,7 @@
             settle(xb.at[k, pl.ds(2, 4)], x_rs.at[k, 2])
             own[k, x, :, 0:4] = own[k, x, :, 0:4] + xb[k, 3] + xb[k, 4]
             own[k, x, :, 4:8] = own[k, x, :, 4:8] + xb[k, 2] + xb[k, 5]
-            if k in Y_THEN_Z:
+            if (c, k) in Y_THEN_Z:
                 for d in (4, 3, 5, 2, 6, 1, 7):
                     src = own.at[k, x, :, lax.rem(y + d, NY)]
                     send(src, yz.at[k, d - 1], yz_ss.at[k], yz_rs.at[k], at(dline=2 * d))
@@ -209,7 +209,7 @@
             finish.append((yr.at[k], y_ss.at[k]))
 
         def e5(k):
-            if k in Y_THEN_Z:
+            if (c, k) in Y_THEN_Z:
                 settle(yz.at[k], yz_rs.at[k])
                 total = own[k, x, :, y]
                 for d in range(1, NY):
@@ -225,7 +225,7 @@
             to_y(k)
 
         def e6(k):
-            if k in Y_THEN_Z and (c, k) != (1, 1):
+            if (c, k) in Y_THEN_Z:
                 settle(yzz.at[k], z_rs.at[k])
                 ag[line, k] = own[k, x, z, y] + yzz[k, 0] + yzz[k, 1] + yzz[k, 2]
                 return
@@ -336,11 +336,11 @@
             e4(1)
             b2(2)
             e5(0)
+            e5(1)
             b3(2)
-            e5(1)
-            b4(2)
             e6(0)
             e6(1)
+            b4(2)
         else:
             ag[line, 2] = jnp.zeros(TILE, F32)
             a1(1)

time: 47.9 us -> 48.2 us (level)
  no operation moved by 1% of the time
where the time goes in v5:
time: 48.2 us; the launch traced here: 48 us
  Pallas kernels  46.7 us (97%)
  between operations  1.28 us (3%)
    pallas_call x1, Pallas kernels, on_device(): pl.pallas_call(functools.partial(kernel, float(entries)), out_shape=shape...  45.8 us

profile of v5, /device:TPU:1, one launch (start us, length us, event | category | flops | bytes accessed | tf_op | source)
XLA Modules:
  0.0 48.0 jit_solution(7292833207477679399)
XLA Ops:
  1.3 45.8 %grad_reduce.1 = (f32[1,32,1280]{2,1,0:T(8,128)S(1)}, bf16[1,768,512]{2,1,0:T(8,128)(2,1)S(1)}) custom-call(s32[1,1,1]{2,1,0:T(1,128)S(6)} %copy.6.cnt, bf16[1,768,512]{2,1,0:T(8,128)(2,1)} %act_hbm.1, bf16[1,768,1280]{2,1,0:T(8,128)(2,1)} %dy_hbm.1, bf16[1,512,1280]{2,1,0:T(8,128)(2,1)} %w_hbm.1), custom_call_target="tpu_custom_call" | custom-call | tf_op jit(solution)/shard_map/grad_reduce/pallas_call | solution.py:445
  47.1 1.0 %store.1 = (f32[1,32,1280]{2,1,0:T(8,128)}, bf16[1,768,512]{2,1,0:T(8,128)(2,1)}) custom-call(f32[1,32,1280]{2,1,0:T(8,128)S(1)} %get-tuple-element.4.a_ref, bf16[1,768,512]{2,1,0:T(8,128)(2,1)S(1)} %get-tuple-element.5.b_ref), custom_call_target="tpu_custom_call" | custom-call | tf_op jit(solution)/shard_map/store/pallas_call | solution.py:456
